TPU v7x, 32 devices: a whole 2x2x4 slice. The times are simulated.
32 devices in a mesh: ctx: 8 (over y, x, core), wt: 4 (over z).
Axes of the slice: x: 2, y: 2, z: 4, core: 2. Of those that a mesh axis runs over, the one named last changes fastest.
Arguments:
- words: bfloat16 [6144, 512], P(('ctx', 'wt')), may hold values from -6 to 6
- teacher: bfloat16 [6144, 512], P(('ctx', 'wt')), may hold values from -6 to 6
- valid: int32 [6144], P(('ctx', 'wt')), may hold values from 0 to 1, as said below
- lengths: int32 [4], replicated, may hold values from 384 to 3072, as said below
- deal: int32 [32], replicated, may hold values from 0 to 31, as said below
- gain_attn: bfloat16 [512], P('wt'), may hold values from 0.25 to 1.75
- shift_attn: bfloat16 [512], P('wt'), may hold values from -3 to 3
- w_qkv: bfloat16 [512, 1536], P('wt'), may hold values from -0.25 to 0.25
- w_out: bfloat16 [512, 512], P('wt'), may hold values from -2 to 2
- gain_mlp: bfloat16 [512], P('wt'), may hold values from 0.25 to 1.75
- shift_mlp: bfloat16 [512], P('wt'), may hold values from -3 to 3
- w_up: bfloat16 [512, 2048], P('wt'), may hold values from -0.25 to 0.25
- w_down: bfloat16 [2048, 512], P('wt'), may hold values from -0.125 to 0.125
Outputs:
- layer_out: bfloat16 [6144, 512], P(('ctx', 'wt'))
- loss: float32 [], replicated
- grad_words: float32 [6144, 512], P(('ctx', 'wt'))
- grad_gain_attn: float32 [512], P('wt')
- grad_shift_attn: float32 [512], P('wt')
- grad_w_qkv: float32 [512, 1536], P('wt')
- grad_w_out: float32 [512, 512], P('wt')
- grad_gain_mlp: float32 [512], P('wt')
- grad_shift_mlp: float32 [512], P('wt')
- grad_w_up: float32 [512, 2048], P('wt')
- grad_w_down: float32 [2048, 512], P('wt')
Inputs may be any that keep to these rules, and one draw needn't show every extreme that they name: lengths are multiples of 192 that sum to 6144; one sequence has exactly 3072 words. `deal`: each initial block appears once; initial blocks that differ by a multiple of the number of ctx indices lie on the same ctx index. The first word of every dealt block is valid.
All inputs are finite; a program needn't handle non-finite values.
Results may differ from a plain program's by a relative error of at most 0.02.
Values may be sent and summed in bfloat16 or wider, within the bound.
No kernel may reach another device: no remote copies, remote signals or barrier semaphores. Data moves between devices by JAX's collectives and lax.ppermute only.
A program may use at most 128 MiB of HBM per device.

v0:
```python
import jax
import jax.numpy as jnp
from jax import lax
from jax.sharding import PartitionSpec as P

H = 8
HEAD = 64
EPS = 1e-05
LOSS_SCALE = 262144.0


def norm_forward(values, gain_vec, shift_vec):
    center = values - jnp.mean(values, axis=-1, keepdims=True)
    inverse = lax.rsqrt(jnp.mean(center * center, axis=-1, keepdims=True) + EPS)
    unit_rows = center * inverse
    return (unit_rows * gain_vec + shift_vec, unit_rows, inverse)


def norm_backward(upstream, unit_rows, inverse, gain_vec):
    scaled = upstream * gain_vec
    inner_term = jnp.mean(scaled * unit_rows, axis=-1, keepdims=True)
    result = inverse * (scaled - jnp.mean(scaled, axis=-1, keepdims=True) - unit_rows * inner_term)
    return (result, jnp.sum(upstream * unit_rows, axis=0), jnp.sum(upstream, axis=0))


def per_device(
    words,
    teacher,
    valid,
    lengths,
    deal,
    gain_attn,
    shift_attn,
    w_qkv,
    w_out,
    gain_mlp,
    shift_mlp,
    w_up,
    w_down,
):
    ctx_count = lax.axis_size("ctx")
    wt_count = lax.axis_size("wt")
    blk_rows = words.shape[0]
    model_width = words.shape[1]
    head_count = H // wt_count
    col_span = 3 * head_count * HEAD
    group_rows = blk_rows * wt_count
    score_scale = HEAD ** (-0.5)
    qkv_full, out_full, gain_first_raw, shift_first_raw = (
        lax.all_gather(w_qkv, "wt", axis=0, tiled=True),
        lax.all_gather(w_out, "wt", axis=0, tiled=True),
        lax.all_gather(gain_attn, "wt", axis=0, tiled=True),
        lax.all_gather(shift_attn, "wt", axis=0, tiled=True),
    )
    qkv_grouped = qkv_full.reshape(model_width, wt_count, col_span)
    out_grouped = out_full.reshape(wt_count, head_count * HEAD, model_width)
    gain_first = gain_first_raw.astype(jnp.float32)
    shift_first = shift_first_raw.astype(jnp.float32)
    inputs = words.astype(jnp.float32)
    normed_one, unit_first, inverse_first = norm_forward(inputs, gain_first, shift_first)
    packed_first = normed_one.astype(jnp.bfloat16)
    projected = jnp.einsum(
        "rd,dwc->wrc", packed_first, qkv_grouped, preferred_element_type=jnp.float32
    ).astype(jnp.bfloat16)
    head_rows = lax.all_to_all(
        projected.reshape(wt_count, blk_rows * col_span),
        "wt",
        split_axis=0,
        concat_axis=0,
        tiled=True,
    )
    head_rows = head_rows.reshape(group_rows, head_count, 3, HEAD)
    queries = head_rows[:, :, 0]
    own_kv = head_rows[:, :, 1:]
    key_values = own_kv.reshape(group_rows, head_count * 2 * HEAD)
    gathered = lax.all_gather(key_values, "ctx", axis=0, tiled=True).reshape(
        ctx_count, group_rows, head_count, 2, HEAD
    )
    offsets = jnp.arange(blk_rows, dtype=jnp.int32)
    bounds = jnp.cumsum(lengths)
    key_place = (deal[:, None] * blk_rows + offsets[None, :]).reshape(ctx_count, group_rows)
    key_seq = jnp.sum((key_place[:, :, None] >= bounds[None, None, :]).astype(jnp.int32), axis=-1)
    ctx_here = lax.axis_index("ctx")
    query_place = lax.dynamic_index_in_dim(key_place, ctx_here, 0, keepdims=False)
    query_seq = lax.dynamic_index_in_dim(key_seq, ctx_here, 0, keepdims=False)
    live_pieces = jnp.ones((ctx_count,), dtype=bool)
    scan_items = (gathered, key_place, key_seq, live_pieces)

    def scores_of(kv_piece, piece_place, piece_seq):
        raw_scores = (
            jnp.einsum(
                "qhd,khd->hqk", queries, kv_piece[:, :, 0], preferred_element_type=jnp.float32
            )
            * score_scale
        )
        visible = (piece_seq[None, :] == query_seq[:, None]) & (
            piece_place[None, :] <= query_place[:, None]
        )
        return (raw_scores, visible[None])

    def forward_step(carry, item):
        kv_piece, piece_place, piece_seq, live_piece = item
        running_max, running_sum, running_acc = carry
        raw_scores, visible = scores_of(kv_piece, piece_place, piece_seq)
        piece_max = jnp.max(jnp.where(visible, raw_scores, -1e30), axis=-1)
        new_max = jnp.maximum(running_max, piece_max)
        weights = jnp.where(visible, jnp.exp(raw_scores - new_max[..., None]), 0.0)
        factor = jnp.exp(running_max - new_max)
        new_sum = running_sum * factor + jnp.sum(weights, axis=-1)
        new_acc = running_acc * factor.T[:, :, None] + jnp.einsum(
            "hqk,khd->qhd",
            weights.astype(jnp.bfloat16),
            kv_piece[:, :, 1],
            preferred_element_type=jnp.float32,
        )
        return ((new_max, new_sum, new_acc), None)

    start_max = jnp.full((head_count, group_rows), -1e30, jnp.float32)
    start_sum = jnp.zeros((head_count, group_rows), jnp.float32)
    start_acc = jnp.zeros((group_rows, head_count, HEAD), jnp.float32)
    (row_max, row_sum, row_acc), _ = lax.scan(
        forward_step, (start_max, start_sum, start_acc), scan_items
    )
    log_total = row_max + jnp.log(row_sum)
    attended_full = row_acc / row_sum.T[:, :, None]
    attended_heads = attended_full.astype(jnp.bfloat16)
    attended_rows = lax.all_to_all(
        attended_heads.reshape(wt_count, blk_rows * head_count * HEAD),
        "wt",
        split_axis=0,
        concat_axis=0,
        tiled=True,
    ).reshape(wt_count, blk_rows, head_count * HEAD)
    residual_one = inputs + jnp.einsum(
        "wrc,wcd->rd", attended_rows, out_grouped, preferred_element_type=jnp.float32
    )
    up_full, down_full, gain_second_raw, shift_second_raw = (
        lax.all_gather(w_up, "wt", axis=0, tiled=True),
        lax.all_gather(w_down, "wt", axis=0, tiled=True),
        lax.all_gather(gain_mlp, "wt", axis=0, tiled=True),
        lax.all_gather(shift_mlp, "wt", axis=0, tiled=True),
    )
    gain_second = gain_second_raw.astype(jnp.float32)
    shift_second = shift_second_raw.astype(jnp.float32)
    normed_two, unit_second, inverse_second = norm_forward(residual_one, gain_second, shift_second)
    packed_second = normed_two.astype(jnp.bfloat16)
    before_act = jnp.dot(packed_second, up_full, preferred_element_type=jnp.float32)
    activated = jax.nn.gelu(before_act, approximate=False).astype(jnp.bfloat16)
    residual_two = residual_one + jnp.dot(activated, down_full, preferred_element_type=jnp.float32)
    distance = residual_two - teacher.astype(jnp.float32)
    valid_float = valid.astype(jnp.float32)
    count_all, square_all = lax.psum(
        (jnp.sum(valid_float), jnp.sum(valid_float * jnp.sum(distance * distance, axis=-1))),
        ("ctx", "wt"),
    )
    loss_value = square_all / (count_all * model_width)
    grad_two = 2.0 * LOSS_SCALE / (count_all * model_width) * valid_float[:, None] * distance
    grad_branch = grad_two.astype(jnp.bfloat16)
    grad_down = jnp.einsum("rf,rd->fd", activated, grad_branch, preferred_element_type=jnp.float32)
    grad_act = jnp.einsum("rd,fd->rf", grad_branch, down_full, preferred_element_type=jnp.float32)
    _, gelu_back = jax.vjp(lambda hidden_in: jax.nn.gelu(hidden_in, approximate=False), before_act)
    grad_pre = gelu_back(grad_act)[0].astype(jnp.bfloat16)
    grad_up = jnp.einsum("rd,rf->df", packed_second, grad_pre, preferred_element_type=jnp.float32)
    grad_normed_two = jnp.einsum("rf,df->rd", grad_pre, up_full, preferred_element_type=jnp.float32)
    back_two, grad_gain_second, grad_shift_second = norm_backward(
        grad_normed_two, unit_second, inverse_second, gain_second
    )
    grad_one = grad_two + back_two
    grad_attn_out = grad_one.astype(jnp.bfloat16)
    grad_out = jnp.einsum(
        "wrc,rd->wcd", attended_rows, grad_attn_out, preferred_element_type=jnp.float32
    ).reshape(model_width, model_width)
    grad_att_rows = jnp.einsum(
        "rd,wcd->wrc", grad_attn_out, out_grouped, preferred_element_type=jnp.float32
    ).astype(jnp.bfloat16)
    grad_att_heads = lax.all_to_all(
        grad_att_rows.reshape(wt_count, blk_rows * head_count * HEAD),
        "wt",
        split_axis=0,
        concat_axis=0,
        tiled=True,
    ).reshape(group_rows, head_count, HEAD)
    row_delta = jnp.sum(grad_att_heads.astype(jnp.float32) * attended_full, axis=-1).T

    def score_grads(kv_piece, piece_place, piece_seq):
        raw_scores, visible = scores_of(kv_piece, piece_place, piece_seq)
        probs = jnp.where(visible, jnp.exp(raw_scores - log_total[..., None]), 0.0)
        grad_probs = jnp.einsum(
            "qhd,khd->hqk", grad_att_heads, kv_piece[:, :, 1], preferred_element_type=jnp.float32
        )
        return (probs, (probs * (grad_probs - row_delta[..., None])).astype(jnp.bfloat16))

    def grad_step(carry, item):
        kv_piece, piece_place, piece_seq, live_piece = item
        probs, grad_scores = score_grads(kv_piece, piece_place, piece_seq)
        grad_keys = (
            jnp.einsum("hqk,qhd->khd", grad_scores, queries, preferred_element_type=jnp.float32)
            * score_scale
        )
        grad_values = jnp.einsum(
            "hqk,qhd->khd",
            probs.astype(jnp.bfloat16),
            grad_att_heads,
            preferred_element_type=jnp.float32,
        )
        grad_next = carry + jnp.einsum(
            "hqk,khd->qhd", grad_scores, kv_piece[:, :, 0], preferred_element_type=jnp.float32
        )
        return (grad_next, jnp.stack([grad_keys, grad_values], axis=2))

    grad_query_sum, grad_pieces = lax.scan(
        grad_step, jnp.zeros((group_rows, head_count, HEAD), jnp.float32), scan_items
    )
    grad_kv = lax.psum_scatter(
        grad_pieces.reshape(ctx_count * group_rows, head_count * 2 * HEAD).astype(jnp.bfloat16),
        "ctx",
        scatter_dimension=0,
        tiled=True,
    ).astype(jnp.float32)
    grad_kv = grad_kv.astype(jnp.bfloat16).reshape(group_rows, head_count, 2, HEAD)
    grad_queries = (grad_query_sum * score_scale).astype(jnp.bfloat16)
    grad_heads = jnp.concatenate([grad_queries[:, :, None], grad_kv], axis=2)
    grad_rows = lax.all_to_all(
        grad_heads.reshape(wt_count, blk_rows * col_span),
        "wt",
        split_axis=0,
        concat_axis=0,
        tiled=True,
    ).reshape(wt_count, blk_rows, col_span)
    grad_qkv = jnp.einsum(
        "rd,wrc->dwc", packed_first, grad_rows, preferred_element_type=jnp.float32
    ).reshape(model_width, 3 * model_width)
    grad_normed_one = jnp.einsum(
        "wrc,dwc->rd", grad_rows, qkv_grouped, preferred_element_type=jnp.float32
    )
    back_one, grad_gain_first, grad_shift_first = norm_backward(
        grad_normed_one, unit_first, inverse_first, gain_first
    )
    grad_words = grad_one + back_one
    shard_ga, shard_sa, shard_qkv, shard_out, shard_gm, shard_sm, shard_up, shard_down = (
        lax.psum_scatter(
            grad_gain_first.astype(jnp.bfloat16), "wt", scatter_dimension=0, tiled=True
        ).astype(jnp.float32),
        lax.psum_scatter(
            grad_shift_first.astype(jnp.bfloat16), "wt", scatter_dimension=0, tiled=True
        ).astype(jnp.float32),
        lax.psum_scatter(
            grad_qkv.astype(jnp.bfloat16), "wt", scatter_dimension=0, tiled=True
        ).astype(jnp.float32),
        lax.psum_scatter(
            grad_out.astype(jnp.bfloat16), "wt", scatter_dimension=0, tiled=True
        ).astype(jnp.float32),
        lax.psum_scatter(
            grad_gain_second.astype(jnp.bfloat16), "wt", scatter_dimension=0, tiled=True
        ).astype(jnp.float32),
        lax.psum_scatter(
            grad_shift_second.astype(jnp.bfloat16), "wt", scatter_dimension=0, tiled=True
        ).astype(jnp.float32),
        lax.psum_scatter(
            grad_up.astype(jnp.bfloat16), "wt", scatter_dimension=0, tiled=True
        ).astype(jnp.float32),
        lax.psum_scatter(
            grad_down.astype(jnp.bfloat16), "wt", scatter_dimension=0, tiled=True
        ).astype(jnp.float32),
    )
    summed = (
        lax.psum(shard_ga.astype(jnp.bfloat16), "ctx").astype(jnp.float32),
        lax.psum(shard_sa.astype(jnp.bfloat16), "ctx").astype(jnp.float32),
        lax.psum(shard_qkv.astype(jnp.bfloat16), "ctx").astype(jnp.float32),
        lax.psum(shard_out.astype(jnp.bfloat16), "ctx").astype(jnp.float32),
        lax.psum(shard_gm.astype(jnp.bfloat16), "ctx").astype(jnp.float32),
        lax.psum(shard_sm.astype(jnp.bfloat16), "ctx").astype(jnp.float32),
        lax.psum(shard_up.astype(jnp.bfloat16), "ctx").astype(jnp.float32),
        lax.psum(shard_down.astype(jnp.bfloat16), "ctx").astype(jnp.float32),
    )
    return (
        residual_two.astype(jnp.bfloat16),
        loss_value,
        grad_words,
        summed[0],
        summed[1],
        summed[2],
        summed[3],
        summed[4],
        summed[5],
        summed[6],
        summed[7],
    )


def solution(mesh):
    placed = (
        P(("ctx", "wt"), None),
        P(("ctx", "wt"), None),
        P(("ctx", "wt")),
        P(),
        P(),
        P("wt"),
        P("wt"),
        P("wt", None),
        P("wt", None),
        P("wt"),
        P("wt"),
        P("wt", None),
        P("wt", None),
    )
    return jax.shard_map(
        per_device,
        mesh=mesh,
        in_specs=placed,
        out_specs=(
            P(("ctx", "wt"), None),
            P(),
            P(("ctx", "wt"), None),
            P("wt"),
            P("wt"),
            P("wt", None),
            P("wt", None),
            P("wt"),
            P("wt"),
            P("wt", None),
            P("wt", None),
        ),
        check_vma=False,
    )
```

profile of v0, /device:TPU:0, one launch (start us, length us, event | category | flops | bytes accessed | tf_op | source)
XLA Modules:
  0.0 679.7 jit_solution(10840386280325061220)
XLA Ops:
  9.3 12.7 %all-gather = bf16[4,1,128]{2,1,0:T(2,128)(2,1)S(1)} all-gather(bf16[1,1,128]{2,1,0:T(2,128)(2,1)} %bitcast.256), channel_id=1, replica_groups=mesh['ctx'=8,'wt'=4] {'wt'}, dimensions={0}, use_global_device_ids=true | all-gather | bytes 1280 | tf_op jit(solution)/shard_map/all_gather | solution.py:52
  22.0 7.8 %all-gather.1 = bf16[4,1,128]{2,1,0:T(2,128)(2,1)S(1)} all-gather(bf16[1,1,128]{2,1,0:T(2,128)(2,1)} %bitcast.257), channel_id=1, replica_groups=mesh['ctx'=8,'wt'=4] {'wt'}, dimensions={0}, use_global_device_ids=true | all-gather | bytes 1280 | tf_op jit(solution)/shard_map/all_gather | solution.py:53
  32.0 18.6 %all-gather.9.cloned.1.call-done = bf16[512,1536]{0,1:T(8,128)(2,1)} async-done(((bf16[128,1536]{0,1:T(8,128)(2,1)}), bf16[512,1536]{0,1:T(8,128)(2,1)}) %all-gather.9.cloned.1.call-update) | async-done | bytes 1572880 | tf_op jit(solution)/shard_map/all_gather | solution.py:50
  53.6 4.4 reduce.16
  58.6 18.8 %all_to_all.40 = bf16[4,2,36864]{2,1,0:T(2,128)(2,1)S(1)} all-to-all(bf16[4,2,36864]{2,1,0:T(2,128)(2,1)S(1)} %reshape.330), channel_id=1, replica_groups=mesh['ctx'=8,'wt'=4] {'wt'}, dimensions={0} | all-to-all | bytes 1179648 | tf_op jit(solution)/shard_map/all_to_all | solution.py:65
  90.4 26.7 %all-gather.11.cloned.1.call-done = bf16[6144,256]{0,1:T(8,128)(2,1)} async-done(((bf16[768,256]{0,1:T(8,128)(2,1)}), bf16[6144,256]{0,1:T(8,128)(2,1)}) %all-gather.11.cloned.1.call-update) | async-done | bytes 3145744 | tf_op jit(solution)/shard_map/all_gather | solution.py:76
  122.3 84.7 %while.28 = (s32[]{:T(128)}, f32[2,768]{1,0:T(2,128)S(1)}, f32[2,768]{1,0:T(2,128)S(1)}, f32[768,2,64]{0,2,1:T(8,128)S(1)}, s32[8,768]{1,0:T(8,128)}, /*index=5*...) while((s32[]{:T(128)}, f32[2,768]{1,0:T(2,128)S(1)}, ...), condition=%wide.region_7.8_spmd.clone, body=%wide.region_4.7_spmd.clone.sunk | while | flops 317039616 | bytes 37675172 | solution.py:121
  127.8 3.8 fusion.123
  138.4 3.8 fusion.123
  148.9 3.8 fusion.123
  159.5 3.8 fusion.123
  170.0 4.1 fusion.123
  181.0 3.8 fusion.123
  191.5 3.9 fusion.123
  202.1 3.8 fusion.123
  213.4 4.5 all-to-all-start.1
  217.9 11.3 %all-gather.2 = bf16[4,1,128]{2,1,0:T(2,128)(2,1)S(1)} all-gather(bf16[1,1,128]{2,1,0:T(2,128)(2,1)S(1)} %bitcast.258), channel_id=1, replica_groups=mesh['ctx'=8,'wt'=4] {'wt'}, dimensions={0}, use_global_device_ids=true | all-gather | bytes 1280 | tf_op jit(solution)/shard_map/all_gather | solution.py:140
  229.2 7.7 %all-gather.3 = bf16[4,1,128]{2,1,0:T(2,128)(2,1)S(1)} all-gather(bf16[1,1,128]{2,1,0:T(2,128)(2,1)S(1)} %bitcast.259), channel_id=1, replica_groups=mesh['ctx'=8,'wt'=4] {'wt'}, dimensions={0}, use_global_device_ids=true | all-gather | bytes 1280 | tf_op jit(solution)/shard_map/all_gather | solution.py:141
  236.9 15.2 %all_gather.31 = bf16[512,512]{1,0:T(8,128)(2,1)S(1)} all-gather(bf16[128,512]{1,0:T(8,128)(2,1)S(1)} %copy-done.20), channel_id=1, replica_groups=mesh['ctx'=8,'wt'=4] {'wt'}, dimensions={0}, use_global_device_ids=true | all-gather | bytes 655360 | tf_op jit(solution)/shard_map/all_gather | solution.py:51
  254.2 6.9 %multiply_convert_fusion = (bf16[192,2048]{1,0:T(8,128)(2,1)}, f32[192,2048]{1,0:T(8,128)}, f32[192,2048]{1,0:T(8,128)}) fusion(bf16[512,2048]{1,0:T(8,128)(2,1)} %all-gather.13.cloned.1.call-done, f32[192,512]{1,0:T(8,128)S(1)} %get-tuple-element.400, f32[512]{0:T(512)S(1)} %bitcast.253, f32[512]{0:T(512)S(1)} %bitcast.249, f32[192]{0:T(256)S(1)} %add_rsqrt_fusion, ...), kind=kOutput, calls=%fused_computation.55 | convolution fusion | flops 428703744 | bytes 6428160 | tf_op jit(solution)/shard_map/dot_general | solution.py:147
  264.3 38.9 %all-reduce.4 = (f32[]{:T(128)}, f32[]{:T(128)}) all-reduce(f32[]{:T(128)} %get-tuple-element.324, f32[]{:T(128)} %get-tuple-element.323), channel_id=1, replica_groups=mesh['ctx'=8,'wt'=4] {'ctx','wt'}, use_global_device_ids=true, to_apply=%region_12.13 | all-reduce | flops 2 | bytes 16 | tf_op jit(solution)/shard_map/psum | solution.py:152
  318.0 5.9 all-to-all-done.2
  328.3 66.9 %while.29 = (s32[]{:T(128)}, f32[768,2,64]{0,2,1:T(8,128)S(1)}, bf16[8,768,2,2,64]{1,4,2,3,0:T(8,128)(2,1)}, bf16[8,768,2,2,64]{1,4,2,3,0:T(8,128)(2,1)}, s32[8,...) while((s32[]{:T(128)}, f32[768,2,64]{0,2,1:T(8,128)S(1)}, ...), condition=%wide.region_19.20_spmd.clone, body=%wide.region_18.19_spmd.clone.sunk | while | flops 769720320 | bytes 28011244 | solution.py:211
  409.4 38.5 %reduce-scatter.6.cloned.1.call-done = bf16[768,256]{0,1:T(8,128)(2,1)} async-done(((bf16[6144,256]{0,1:T(8,128)(2,1)}), bf16[768,256]{0,1:T(8,128)(2,1)}) %reduce-scatter.6.cloned.1.call-update) | async-done | bytes 393232 | tf_op jit(solution)/shard_map/reduce_scatter | solution.py:214
  452.1 5.6 reduce.19
  458.3 23.0 %all_to_all.41 = bf16[4,2,36864]{2,1,0:T(2,128)(2,1)S(1)} all-to-all(bf16[4,2,36864]{2,1,0:T(2,128)(2,1)S(1)} %reshape.336), channel_id=1, replica_groups=mesh['ctx'=8,'wt'=4] {'wt'}, dimensions={0} | all-to-all | bytes 1179648 | tf_op jit(solution)/shard_map/all_to_all | solution.py:223
  490.3 31.3 %reduce-scatter.12.cloned.1.call-done = bf16[128,2048]{1,0:T(8,128)(2,1)} async-done(((bf16[512,2048]{1,0:T(8,128)(2,1)}), bf16[128,2048]{1,0:T(8,128)(2,1)}) %reduce-scatter.12.cloned.1.call-update) | async-done | bytes 524304 | tf_op jit(solution)/shard_map/reduce_scatter | solution.py:259
  521.7 45.5 %reduce-scatter.14.cloned.1.call-done = bf16[512,512]{1,0:T(8,128)(2,1)} async-done(((bf16[2048,512]{1,0:T(8,128)(2,1)}), bf16[512,512]{1,0:T(8,128)(2,1)}) %reduce-scatter.14.cloned.1.call-update) | async-done | bytes 524304 | tf_op jit(solution)/shard_map/reduce_scatter | solution.py:262
  567.2 37.1 %reduce-scatter.8.cloned.1.call-done = bf16[128,1536]{1,0:T(8,128)(2,1)} async-done(((bf16[512,1536]{1,0:T(8,128)(2,1)}), bf16[128,1536]{1,0:T(8,128)(2,1)}) %reduce-scatter.8.cloned.1.call-update) | async-done | bytes 393232 | tf_op jit(solution)/shard_map/reduce_scatter | solution.py:247
  606.4 9.8 %all-reduce.7 = (bf16[512]{0:T(512)(128)(2,1)S(1)}, bf16[512]{0:T(512)(128)(2,1)S(1)}, bf16[512]{0:T(512)(128)(2,1)S(1)}, bf16[512]{0:T(512)(128)(2,1)S(1)}) all-reduce(bf16[512]{0:T(512)(128)(2,1)S(1)} %get-tuple-element.317, bf16[512]{0:T(512)(128)(2,1)S(1)} %get-tuple-element.322, ...), channel_id=3, replica_groups=mesh['ctx'=8,'wt'=4] {'wt'}, use_global_device_ids=true, to_apply=%region_24.25.clone | all-reduce | flops 2048 | bytes 8192
  616.5 11.9 %all-reduce.5 = (bf16[128]{0:T(256)(128)(2,1)S(1)}, bf16[128]{0:T(256)(128)(2,1)S(1)}, bf16[128]{0:T(256)(128)(2,1)S(1)}, bf16[128]{0:T(256)(128)(2,1)S(1)}) all-reduce(bf16[128]{0:T(256)(128)(2,1)S(1)} %dynamic-slice.1, bf16[128]{0:T(256)(128)(2,1)S(1)} %dynamic-slice.3, ...), channel_id=1, replica_groups=mesh['ctx'=8,'wt'=4] {'ctx'}, use_global_device_ids=true, to_apply=%region_25.26 | all-reduce | flops 512 | bytes 2048 | tf_op jit(solution)/shard_map/psum | solution.py:267
  631.3 35.2 %all-reduce.10.cloned.1.call-done = (bf16[128,1536]{1,0:T(8,128)(2,1)}, bf16[128,512]{1,0:T(8,128)(2,1)}, bf16[128,2048]{1,0:T(8,128)(2,1)}, bf16[512,512]{1,0:T(8,128)(2,1)}) async-done(((bf16[128,1536]{1,0:T(8,128)(2,1)}, bf16[128,512]{1,0:T(8,128)(2,1)}, bf16[128,2048]{1,0:T(8,128)(2,1)}, bf16[512,512]{1,0:T(8,128)(2,1)}), (bf16[128,1536]{1,0:T(8,128)(2,1)}, bf16[128,512]{1,0:T(8,128)(2,1)}, ...) | async-done | bytes 1572880 | tf_op jit(solution)/shard_map/psum | solution.py:269
  (418 shorter events, 212.1 us)
Async XLA Ops:
  7.2 43.5 %copy-start.3 = (bf16[192,512]{1,0:T(8,128)(2,1)S(1)}, bf16[192,512]{1,0:T(8,128)(2,1)}, u32[]{:S(2)}) copy-start(bf16[192,512]{1,0:T(8,128)(2,1)} %param.17) | copy-start | bytes 589828
  7.2 43.4 %all-gather.9.cloned.1.call-start = ((), (), s32[]{:S(2)}) async-start(), calls=%async_computation.9 | async-start | bytes 1966080 | tf_op jit(solution)/shard_map/all_gather | solution.py:50
  9.2 107.9 %all-gather.11.cloned.1.call-start = ((), (), s32[]{:S(2)}) async-start(), calls=%async_computation.10 | async-start | bytes 3538944 | tf_op jit(solution)/shard_map/all_gather | solution.py:76
  22.0 28.6 %copy-start.22 = (f32[4,1,128]{2,1,0:T(1,128)}, f32[4,1,128]{2,1,0:T(1,128)S(1)}, u32[]{:S(2)}) copy-start(f32[4,1,128]{2,1,0:T(1,128)S(1)} %convert_element_type.187) | copy-start | bytes 6148
  29.8 20.8 %copy-start.26 = (f32[4,1,128]{2,1,0:T(1,128)}, f32[4,1,128]{2,1,0:T(1,128)S(1)}, u32[]{:S(2)}) copy-start(f32[4,1,128]{2,1,0:T(1,128)S(1)} %convert_element_type.188) | copy-start | bytes 6148
  30.8 19.8 %copy-start.24 = (f32[192]{0:T(256)}, f32[192]{0:T(256)S(1)}, u32[]{:S(2)}) copy-start(f32[192]{0:T(256)S(1)} %broadcast_multiply_fusion.5) | copy-start | bytes 2308
  32.0 18.6 %copy-start.32 = (f32[192]{0:T(256)}, f32[192]{0:T(256)S(1)}, u32[]{:S(2)}) copy-start(f32[192]{0:T(256)S(1)} %add_rsqrt_fusion.1) | copy-start | bytes 2308
  85.4 168.8 %all-gather.13.cloned.1.call-start = ((), (), s32[]{:S(2)}) async-start(), calls=%async_computation.11 | async-start | bytes 2621440 | tf_op jit(solution)/shard_map/all_gather | solution.py:138
  86.1 175.0 %all-gather.15.cloned.1.call-start = ((), (), s32[]{:S(2)}) async-start(), calls=%async_computation.12 | async-start | bytes 2621440 | tf_op jit(solution)/shard_map/all_gather | solution.py:139
  138.4 3.8 copy-start
  170.0 4.3 copy-start
  191.5 3.9 copy-start
  210.4 7.5 %copy-start.43 = (bf16[128]{0:T(256)(128)(2,1)S(1)}, bf16[128]{0:T(256)(128)(2,1)}, u32[]{:S(2)}) copy-start(bf16[128]{0:T(256)(128)(2,1)} %param.26) | copy-start | bytes 772
  210.4 18.9 %copy-start.44 = (bf16[128]{0:T(256)(128)(2,1)S(1)}, bf16[128]{0:T(256)(128)(2,1)}, u32[]{:S(2)}) copy-start(bf16[128]{0:T(256)(128)(2,1)} %param.27) | copy-start | bytes 772
  210.4 26.5 %copy-start.20 = (bf16[128,512]{1,0:T(8,128)(2,1)S(1)}, bf16[128,512]{1,0:T(8,128)(2,1)}, u32[]{:S(2)}) copy-start(bf16[128,512]{1,0:T(8,128)(2,1)} %param.25) | copy-start | bytes 393220
  213.4 38.7 %all-to-all-start.1 = ((bf16[4,2,12288]{2,1,0:T(2,128)(2,1)}), bf16[4,2,12288]{2,1,0:T(2,128)(2,1)S(1)}, u32[]{:S(2)}, u32[]{:S(2)}) async-start(bf16[4,2,12288]{2,1,0:T(2,128)(2,1)} %reshape.332), calls=%async_computation.1 | async-start | bytes 393216 | tf_op jit(solution)/shard_map/all_to_all | solution.py:127
  229.2 80.0 %copy-start.28 = (f32[4,1,128]{2,1,0:T(1,128)}, f32[4,1,128]{2,1,0:T(1,128)S(1)}, u32[]{:S(2)}) copy-start(f32[4,1,128]{2,1,0:T(1,128)S(1)} %convert_element_type.189) | copy-start | bytes 6148
  236.9 17.3 %copy-start.36 = (f32[4,1,128]{2,1,0:T(1,128)}, f32[4,1,128]{2,1,0:T(1,128)S(1)}, u32[]{:S(2)}) copy-start(f32[4,1,128]{2,1,0:T(1,128)S(1)} %convert_element_type.190) | copy-start | bytes 6148
  253.5 7.6 %copy-start.8 = (bf16[4,24576]{1,0:T(4,128)(2,1)}, bf16[4,24576]{1,0:T(4,128)(2,1)S(1)}, u32[]{:S(2)}) copy-start(bf16[4,24576]{1,0:T(4,128)(2,1)S(1)} %reduce.7) | copy-start | bytes 589828
  253.9 55.3 %copy-start.1 = (f32[192,512]{1,0:T(8,128)}, f32[192,512]{1,0:T(8,128)S(1)}, u32[]{:S(2)}) copy-start(f32[192,512]{1,0:T(8,128)S(1)} %get-tuple-element.400) | copy-start | bytes 1179652
  253.9 55.3 %copy-start.30 = (f32[192]{0:T(256)}, f32[192]{0:T(256)S(1)}, u32[]{:S(2)}) copy-start(f32[192]{0:T(256)S(1)} %broadcast_multiply_fusion.4) | copy-start | bytes 2308
  254.1 55.1 %copy-start.34 = (f32[192]{0:T(256)}, f32[192]{0:T(256)S(1)}, u32[]{:S(2)}) copy-start(f32[192]{0:T(256)S(1)} %add_rsqrt_fusion) | copy-start | bytes 2308
  254.2 6.9 %copy-start.7 = (bf16[192,512]{1,0:T(8,128)(2,1)S(1)}, bf16[192,512]{1,0:T(8,128)(2,1)}, u32[]{:S(2)}) copy-start(bf16[192,512]{1,0:T(8,128)(2,1)} %param.18) | copy-start | bytes 589828
  310.1 13.9 %copy-start.4 = (f32[192,512]{1,0:T(8,128)}, f32[192,512]{1,0:T(8,128)S(1)}, u32[]{:S(2)}) copy-start(f32[192,512]{1,0:T(8,128)S(1)} %get-tuple-element.395) | copy-start | bytes 1179652
  310.1 7.2 %copy-start.18 = (f32[2,768]{1,0:T(2,128)S(1)}, f32[2,768]{1,0:T(2,128)}, u32[]{:S(2)}) copy-start(f32[2,768]{1,0:T(2,128)} %copy-done.17) | copy-start | bytes 18436
  313.3 10.5 %all-to-all-start.2 = ((bf16[4,2,12288]{2,1,0:T(2,128)(2,1)}), bf16[4,2,12288]{2,1,0:T(2,128)(2,1)S(1)}, u32[]{:S(2)}, u32[]{:S(2)}) async-start(bf16[4,2,12288]{2,1,0:T(2,128)(2,1)} %reshape.334), calls=%async_computation.2 | async-start | bytes 393216 | tf_op jit(solution)/shard_map/all_to_all | solution.py:176
  317.1 130.7 %reduce-scatter.6.cloned.1.call-start = ((), (), s32[]{:S(2)}) async-start(), calls=%async_computation.13 | async-start | bytes 3538944 | tf_op jit(solution)/shard_map/reduce_scatter | solution.py:214
  401.5 88.9 %reduce-scatter.10.cloned.1.call-start = ((), (), s32[]{:S(2)}) async-start(), calls=%async_computation.15 | async-start | bytes 655360 | tf_op jit(solution)/shard_map/reduce_scatter | solution.py:250
  403.6 118.1 %reduce-scatter.12.cloned.1.call-start = ((), (), s32[]{:S(2)}) async-start(), calls=%async_computation.16 | async-start | bytes 2621440 | tf_op jit(solution)/shard_map/reduce_scatter | solution.py:259
  405.9 161.3 %reduce-scatter.14.cloned.1.call-start = ((), (), s32[]{:S(2)}) async-start(), calls=%async_computation.17 | async-start | bytes 2621440 | tf_op jit(solution)/shard_map/reduce_scatter | solution.py:262
  409.3 195.0 %reduce-scatter.8.cloned.1.call-start = ((), (), s32[]{:S(2)}) async-start(), calls=%async_computation.14 | async-start | bytes 1966080 | tf_op jit(solution)/shard_map/reduce_scatter | solution.py:247
  488.4 178.2 %all-reduce.10.cloned.1.call-start = ((), (), s32[]{:S(2)}) async-start(), calls=%async_computation.18 | async-start | bytes 3145728 | tf_op jit(solution)/shard_map/psum | solution.py:269
  (57 other events, 97.6 us)
Sparse Core Ops, SparseCore 0:
  10.2 40.4 all-gather.8
  85.5 31.5 all-gather.10
  118.7 45.9 all-gather.12
  166.1 44.6 all-gather.14
  401.5 46.3 reduce-scatter.5
  450.7 23.8 reduce-scatter.9
  477.0 44.6 reduce-scatter.11
  523.9 43.1 reduce-scatter.13
  569.6 34.5 reduce-scatter.7
  608.1 58.3 all-reduce.9
where the time goes:
time: 687 us; the launch traced here: 680 us
  waiting for transfers between devices  240 us (35%)
  blocking collectives  157 us (23%)
  matrix products  124 us (18%)
  local copies, waits for them, and re-layouts  65.7 us (10%)
  other arithmetic  64.5 us (9%)
  between operations  18.4 us (3%)
  starting transfers between devices  9.25 us (1%)
    reduce_scatter x1, waiting for transfers between devices, per_device(): lax.psum_scatter(grad_down.astype(jnp.bfloat16), 'wt', scatter_dimension=...  45.5 us
    psum x1, blocking collectives, per_device(): lax.psum((jnp.sum(valid_float), jnp.sum(valid_float * jnp.sum(distance *...  38.9 us
    reduce_scatter x1, waiting for transfers between devices, per_device(): lax.psum_scatter(grad_pieces.reshape(ctx_count * group_rows, head_count *...  38.5 us
    reduce_scatter x1, waiting for transfers between devices, per_device(): lax.psum_scatter(grad_qkv.astype(jnp.bfloat16), 'wt', scatter_dimension=0...  37.1 us
    psum x1, waiting for transfers between devices, per_device(): lax.psum(shard_qkv.astype(jnp.bfloat16), 'ctx').astype(jnp.float32)  35.2 us
    dot_general x16, matrix products, scores_of(): jnp.einsum('qhd,khd->hqk', queries, kv_piece[:, :, 0], preferred_element_...  32 us
    reduce_scatter x1, waiting for transfers between devices, per_device(): lax.psum_scatter(grad_up.astype(jnp.bfloat16), 'wt', scatter_dimension=0,...  31.3 us
    dot_general x8, matrix products, forward_step(): jnp.einsum('hqk,khd->qhd', weights.astype(jnp.bfloat16), kv_piece[:, :, 1...  30.9 us
  transfers between devices with their start and end apart: 12, of which 8 were waited for; matrix products, arithmetic and copies ran while one was open for 20% of the time, Pallas kernels for 0%

commit v1 on v0

--- a/solution.py
+++ b/solution.py
@@ -266,7 +266,7 @@
     summed = (
         lax.psum(shard_ga.astype(jnp.bfloat16), "ctx").astype(jnp.float32),
         lax.psum(shard_sa.astype(jnp.bfloat16), "ctx").astype(jnp.float32),
-        lax.psum(shard_qkv.astype(jnp.bfloat16), "ctx").astype(jnp.float32),
+        jnp.sum(lax.all_gather(shard_qkv.astype(jnp.bfloat16), "ctx"), axis=0).astype(jnp.float32),
         lax.psum(shard_out.astype(jnp.bfloat16), "ctx").astype(jnp.float32),
         lax.psum(shard_gm.astype(jnp.bfloat16), "ctx").astype(jnp.float32),
         lax.psum(shard_sm.astype(jnp.bfloat16), "ctx").astype(jnp.float32),

time: 687 us -> 709 us (1.032)
  matrix products: 124 us -> 88.4 us
  waiting for transfers between devices: 240 us -> 265 us
  other arithmetic: 64.5 us -> 80.1 us
  blocking collectives: 157 us -> 169 us
    psum x1, waiting for transfers between devices: 35.2 us -> 58.3 us  [per_device(): lax.psum(shard_out.astype(jnp.bfloat16), 'ctx').astype(jnp.float32)]
    dot_general x8, matrix products: 30.9 us -> 10.7 us  [forward_step(): jnp.einsum('hqk,khd->qhd', weights.astype(jnp.bfloat16), kv_piece[:, :, 1...]
    dot_general x16, matrix products: 32 us -> 15.2 us  [scores_of(): jnp.einsum('qhd,khd->hqk', queries, kv_piece[:, :, 0], preferred_element_...]
    squeeze x16, local copies, waits for them, and re-layouts: 16.5 us -> 0.56 us  [per_device(): lax.scan(forward_step, (start_max, start_sum, start_acc), scan_items)]
    unnamed x110 -> x106, local copies, waits for them, and re-layouts: 20.2 us -> 28.7 us
  transfers between devices with their start and end apart: 12 -> 13, of which waited for: 8 -> 9; matrix products, arithmetic and copies ran while one was open for 20% -> 15% of each run, Pallas kernels for 0% -> 0%
where the time goes in v1:
time: 709 us; the launch traced here: 701 us
  waiting for transfers between devices  265 us (37%)
  blocking collectives  169 us (24%)
  matrix products  88.4 us (12%)
  other arithmetic  80.1 us (11%)
  local copies, waits for them, and re-layouts  69.1 us (10%)
  between operations  18 us (3%)
  starting transfers between devices  9.64 us (1%)
    psum x1, waiting for transfers between devices, per_device(): lax.psum(shard_out.astype(jnp.bfloat16), 'ctx').astype(jnp.float32)  58.3 us
    reduce_scatter x1, waiting for transfers between devices, per_device(): lax.psum_scatter(grad_down.astype(jnp.bfloat16), 'wt', scatter_dimension=...  45.5 us
    psum x1, blocking collectives, per_device(): lax.psum((jnp.sum(valid_float), jnp.sum(valid_float * jnp.sum(distance *...  38.5 us
    reduce_scatter x1, waiting for transfers between devices, per_device(): lax.psum_scatter(grad_qkv.astype(jnp.bfloat16), 'wt', scatter_dimension=0...  37 us
    reduce_scatter x1, waiting for transfers between devices, per_device(): lax.psum_scatter(grad_pieces.reshape(ctx_count * group_rows, head_count *...  36.5 us
    reduce_scatter x1, waiting for transfers between devices, per_device(): lax.psum_scatter(grad_up.astype(jnp.bfloat16), 'wt', scatter_dimension=0,...  33.9 us
    unnamed x106, local copies, waits for them, and re-layouts  28.7 us
    all_gather x1, waiting for transfers between devices, per_device(): lax.all_gather(key_values, 'ctx', axis=0, tiled=True)  28 us
  transfers between devices with their start and end apart: 13, of which 9 were waited for; matrix products, arithmetic and copies ran while one was open for 15% of the time, Pallas kernels for 0%

profile of v1, /device:TPU:0, one launch (start us, length us, event | category | flops | bytes accessed | tf_op | source)
XLA Modules:
  0.0 701.3 jit_solution(15469828185903130465)
XLA Ops:
  9.3 12.7 %all-gather.1 = bf16[4,1,128]{2,1,0:T(2,128)(2,1)S(1)} all-gather(bf16[1,1,128]{2,1,0:T(2,128)(2,1)} %bitcast.258), channel_id=1, replica_groups=mesh['ctx'=8,'wt'=4] {'wt'}, dimensions={0}, use_global_device_ids=true | all-gather | bytes 1280 | tf_op jit(solution)/shard_map/all_gather | solution.py:52
  22.0 7.8 %all-gather.2 = bf16[4,1,128]{2,1,0:T(2,128)(2,1)S(1)} all-gather(bf16[1,1,128]{2,1,0:T(2,128)(2,1)} %bitcast.259), channel_id=1, replica_groups=mesh['ctx'=8,'wt'=4] {'wt'}, dimensions={0}, use_global_device_ids=true | all-gather | bytes 1280 | tf_op jit(solution)/shard_map/all_gather | solution.py:53
  32.0 18.6 %all-gather.11.cloned.1.call-done = bf16[512,1536]{0,1:T(8,128)(2,1)} async-done(((bf16[128,1536]{0,1:T(8,128)(2,1)}), bf16[512,1536]{0,1:T(8,128)(2,1)}) %all-gather.11.cloned.1.call-update) | async-done | bytes 1572880 | tf_op jit(solution)/shard_map/all_gather | solution.py:50
  53.6 4.4 reduce.17
  58.6 18.8 %all_to_all.40 = bf16[4,2,36864]{2,1,0:T(2,128)(2,1)S(1)} all-to-all(bf16[4,2,36864]{2,1,0:T(2,128)(2,1)S(1)} %reshape.331), channel_id=1, replica_groups=mesh['ctx'=8,'wt'=4] {'wt'}, dimensions={0} | all-to-all | bytes 1179648 | tf_op jit(solution)/shard_map/all_to_all | solution.py:65
  78.0 3.8 reduce.7
  89.1 28.0 %all-gather.13.cloned.1.call-done = bf16[6144,256]{0,1:T(8,128)(2,1)} async-done(((bf16[768,256]{0,1:T(8,128)(2,1)}), bf16[6144,256]{0,1:T(8,128)(2,1)}) %all-gather.13.cloned.1.call-update) | async-done | bytes 3145744 | tf_op jit(solution)/shard_map/all_gather | solution.py:76
  120.6 44.8 %while.28 = (s32[]{:T(128)}, f32[2,768]{1,0:T(2,128)S(1)}, f32[2,768]{1,0:T(2,128)}, f32[768,2,64]{0,2,1:T(8,128)}, s32[8,768]{1,0:T(8,128)}, /*index=5*/s32[768...) while((s32[]{:T(128)}, f32[2,768]{1,0:T(2,128)S(1)}, ...), condition=%wide.region_7.8_spmd.clone, body=%wide.region_4.7_spmd.clone.sunk | while | flops 317039616 | bytes 21995776 | solution.py:121
  174.4 3.5 reduce.18
  179.7 4.6 all-to-all-start.1
  184.3 13.2 %all-gather.3 = bf16[4,1,128]{2,1,0:T(2,128)(2,1)S(1)} all-gather(bf16[1,1,128]{2,1,0:T(2,128)(2,1)} %bitcast.260), channel_id=1, replica_groups=mesh['ctx'=8,'wt'=4] {'wt'}, dimensions={0}, use_global_device_ids=true | all-gather | bytes 1280 | tf_op jit(solution)/shard_map/all_gather | solution.py:140
  198.2 11.8 %all-gather.4 = bf16[4,1,128]{2,1,0:T(2,128)(2,1)S(1)} all-gather(bf16[1,1,128]{2,1,0:T(2,128)(2,1)} %bitcast.261), channel_id=1, replica_groups=mesh['ctx'=8,'wt'=4] {'wt'}, dimensions={0}, use_global_device_ids=true | all-gather | bytes 1280 | tf_op jit(solution)/shard_map/all_gather | solution.py:141
  210.5 17.1 %all_gather.37 = bf16[512,512]{1,0:T(8,128)(2,1)} all-gather(bf16[128,512]{1,0:T(8,128)(2,1)} %param.25), channel_id=1, replica_groups=mesh['ctx'=8,'wt'=4] {'wt'}, dimensions={0}, use_global_device_ids=true | all-gather | bytes 655360 | tf_op jit(solution)/shard_map/all_gather | solution.py:51
  235.7 7.3 %multiply_convert_fusion = (bf16[192,2048]{1,0:T(8,128)(2,1)}, f32[192,2048]{1,0:T(8,128)}, f32[192,2048]{1,0:T(8,128)}) fusion(bf16[512,2048]{1,0:T(8,128)(2,1)} %all-gather.15.cloned.1.call-done, f32[192,512]{1,0:T(8,128)} %copy-done.3, f32[512]{0:T(512)} %bitcast.255, f32[512]{0:T(512)} %bitcast.251, f32[192]{0:T(256)} %add_rsqrt_fusion, f32[192]{0:T(256)} %copy-done.35), kind=kOutput, calls=%fused_computation.55 | convolution fusion | flops 428703744 | bytes 6428160 | tf_op jit(solution)/shard_map/dot_general | solution.py:147
  243.1 3.3 multiply_reduce_fusion.3
  246.9 38.5 %all-reduce.4 = (f32[]{:T(128)}, f32[]{:T(128)}) all-reduce(f32[]{:T(128)} %get-tuple-element.324, f32[]{:T(128)} %get-tuple-element.323), channel_id=1, replica_groups=mesh['ctx'=8,'wt'=4] {'ctx','wt'}, use_global_device_ids=true, to_apply=%region_12.13 | all-reduce | flops 2 | bytes 16 | tf_op jit(solution)/shard_map/psum | solution.py:152
  288.1 3.7 add_convert_fusion
  298.0 3.5 reduce.19
  303.4 4.0 all-to-all-start.2
  308.9 5.8 all-to-all-done.2
  328.4 59.1 %while.29 = (s32[]{:T(128)}, f32[768,2,64]{0,2,1:T(8,128)}, bf16[8,768,2,2,64]{1,4,2,3,0:T(8,128)(2,1)}, bf16[8,768,2,2,64]{1,4,2,3,0:T(8,128)(2,1)S(1)}, s32[8,...) while((s32[]{:T(128)}, f32[768,2,64]{0,2,1:T(8,128)}, ...), condition=%wide.region_19.20_spmd.clone, body=%wide.region_18.19_spmd.clone.sunk | while | flops 769720320 | bytes 31156524 | solution.py:211
  387.5 3.6 copy.129
  402.8 36.5 %reduce-scatter.6.cloned.1.call-done = bf16[768,256]{0,1:T(8,128)(2,1)} async-done(((bf16[6144,256]{0,1:T(8,128)(2,1)}), bf16[768,256]{0,1:T(8,128)(2,1)}) %reduce-scatter.6.cloned.1.call-update) | async-done | bytes 393232 | tf_op jit(solution)/shard_map/reduce_scatter | solution.py:214
  442.4 4.4 reduce.20
  447.5 25.3 %all_to_all.41 = bf16[4,2,36864]{2,1,0:T(2,128)(2,1)S(1)} all-to-all(bf16[4,2,36864]{2,1,0:T(2,128)(2,1)S(1)} %reshape.337), channel_id=1, replica_groups=mesh['ctx'=8,'wt'=4] {'wt'}, dimensions={0} | all-to-all | bytes 1179648 | tf_op jit(solution)/shard_map/all_to_all | solution.py:223
  473.3 3.8 reduce.10
  479.8 33.9 %reduce-scatter.12.cloned.1.call-done = bf16[128,2048]{1,0:T(8,128)(2,1)} async-done(((bf16[512,2048]{1,0:T(8,128)(2,1)}), bf16[128,2048]{1,0:T(8,128)(2,1)}) %reduce-scatter.12.cloned.1.call-update) | async-done | bytes 524304 | tf_op jit(solution)/shard_map/reduce_scatter | solution.py:259
  513.7 45.5 %reduce-scatter.14.cloned.1.call-done = bf16[512,512]{1,0:T(8,128)(2,1)} async-done(((bf16[2048,512]{1,0:T(8,128)(2,1)}), bf16[512,512]{1,0:T(8,128)(2,1)}) %reduce-scatter.14.cloned.1.call-update) | async-done | bytes 524304 | tf_op jit(solution)/shard_map/reduce_scatter | solution.py:262
  559.2 37.0 %reduce-scatter.8.cloned.1.call-done = bf16[128,1536]{1,0:T(8,128)(2,1)} async-done(((bf16[512,1536]{1,0:T(8,128)(2,1)}), bf16[128,1536]{1,0:T(8,128)(2,1)}) %reduce-scatter.8.cloned.1.call-update) | async-done | bytes 393232 | tf_op jit(solution)/shard_map/reduce_scatter | solution.py:247
  598.2 58.3 %all-reduce.10.cloned.1.call-done = (bf16[128,512]{1,0:T(8,128)(2,1)}, bf16[128,2048]{1,0:T(8,128)(2,1)}, bf16[512,512]{1,0:T(8,128)(2,1)}) async-done(((bf16[128,512]{1,0:T(8,128)(2,1)}, bf16[128,2048]{1,0:T(8,128)(2,1)}, bf16[512,512]{1,0:T(8,128)(2,1)}), (bf16[128,512]{1,0:T(8,128)(2,1)}, bf16[128,2048]{1,0:T(8,128)(2,1)}, bf16[512,512]{1,0:T(8,128)(2,1)})) %all-reduce.10.cloned.1.call-update) | async-done | bytes 1179664 | tf_op jit(solution)/shard_map/psum | solution.py:270
  662.2 11.7 %all-reduce.7 = (bf16[512]{0:T(512)(128)(2,1)S(1)}, bf16[512]{0:T(512)(128)(2,1)S(1)}, bf16[512]{0:T(512)(128)(2,1)S(1)}, bf16[512]{0:T(512)(128)(2,1)S(1)}) all-reduce(bf16[512]{0:T(512)(128)(2,1)S(1)} %get-tuple-element.317, bf16[512]{0:T(512)(128)(2,1)S(1)} %get-tuple-element.322, ...), channel_id=4, replica_groups=mesh['ctx'=8,'wt'=4] {'wt'}, use_global_device_ids=true, to_apply=%region_24.25.clone | all-reduce | flops 2048 | bytes 8192
  674.2 12.1 %all-reduce.5 = (bf16[128]{0:T(256)(128)(2,1)S(1)}, bf16[128]{0:T(256)(128)(2,1)S(1)}, bf16[128]{0:T(256)(128)(2,1)S(1)}, bf16[128]{0:T(256)(128)(2,1)S(1)}) all-reduce(bf16[128]{0:T(256)(128)(2,1)S(1)} %dynamic-slice.1, bf16[128]{0:T(256)(128)(2,1)S(1)} %dynamic-slice.3, ...), channel_id=1, replica_groups=mesh['ctx'=8,'wt'=4] {'ctx'}, use_global_device_ids=true, to_apply=%region_25.26 | all-reduce | flops 512 | bytes 2048 | tf_op jit(solution)/shard_map/psum | solution.py:267
  (498 shorter events, 199.1 us)
Async XLA Ops:
  7.2 43.5 %copy-start.6 = (bf16[192,512]{1,0:T(8,128)(2,1)S(1)}, bf16[192,512]{1,0:T(8,128)(2,1)}, u32[]{:S(2)}) copy-start(bf16[192,512]{1,0:T(8,128)(2,1)} %param.17) | copy-start | bytes 589828
  7.2 43.4 %all-gather.11.cloned.1.call-start = ((), (), s32[]{:S(2)}) async-start(), calls=%async_computation.9 | async-start | bytes 1966080 | tf_op jit(solution)/shard_map/all_gather | solution.py:50
  9.2 107.9 %all-gather.13.cloned.1.call-start = ((), (), s32[]{:S(2)}) async-start(), calls=%async_computation.10 | async-start | bytes 3538944 | tf_op jit(solution)/shard_map/all_gather | solution.py:76
  22.0 28.6 %copy-start.27 = (f32[4,1,128]{2,1,0:T(1,128)}, f32[4,1,128]{2,1,0:T(1,128)S(1)}, u32[]{:S(2)}) copy-start(f32[4,1,128]{2,1,0:T(1,128)S(1)} %convert_element_type.189) | copy-start | bytes 6148
  29.8 20.8 %copy-start.31 = (f32[4,1,128]{2,1,0:T(1,128)}, f32[4,1,128]{2,1,0:T(1,128)S(1)}, u32[]{:S(2)}) copy-start(f32[4,1,128]{2,1,0:T(1,128)S(1)} %convert_element_type.190) | copy-start | bytes 6148
  30.8 19.8 %copy-start.29 = (f32[192]{0:T(256)}, f32[192]{0:T(256)S(1)}, u32[]{:S(2)}) copy-start(f32[192]{0:T(256)S(1)} %broadcast_multiply_fusion.5) | copy-start | bytes 2308
  32.0 18.6 %copy-start.38 = (f32[192]{0:T(256)}, f32[192]{0:T(256)S(1)}, u32[]{:S(2)}) copy-start(f32[192]{0:T(256)S(1)} %add_rsqrt_fusion.1) | copy-start | bytes 2308
  83.7 3.1 copy-start.49
  83.7 3.2 copy-start.50
  85.4 150.3 %all-gather.15.cloned.1.call-start = ((), (), s32[]{:S(2)}) async-start(), calls=%async_computation.11 | async-start | bytes 2621440 | tf_op jit(solution)/shard_map/all_gather | solution.py:138
  86.1 156.9 %all-gather.17.cloned.1.call-start = ((), (), s32[]{:S(2)}) async-start(), calls=%async_computation.12 | async-start | bytes 2621440 | tf_op jit(solution)/shard_map/all_gather | solution.py:139
  179.7 47.9 %all-to-all-start.1 = ((bf16[4,2,12288]{2,1,0:T(2,128)(2,1)}), bf16[4,2,12288]{2,1,0:T(2,128)(2,1)}, u32[]{:S(2)}, u32[]{:S(2)}) async-start(bf16[4,2,12288]{2,1,0:T(2,128)(2,1)} %reshape.333), calls=%async_computation.1 | async-start | bytes 393216 | tf_op jit(solution)/shard_map/all_to_all | solution.py:127
  243.1 3.3 copy-start.45
  288.0 3.8 copy-start.15
  288.0 3.8 copy-start.4
  288.0 3.8 copy-start.33
  288.0 3.8 copy-start.36
  288.0 3.8 copy-start.40
  288.1 3.8 copy-start.48
  303.4 11.4 %all-to-all-start.2 = ((bf16[4,2,12288]{2,1,0:T(2,128)(2,1)}), bf16[4,2,12288]{2,1,0:T(2,128)(2,1)}, u32[]{:S(2)}, u32[]{:S(2)}) async-start(bf16[4,2,12288]{2,1,0:T(2,128)(2,1)} %reshape.335), calls=%async_computation.2 | async-start | bytes 393216 | tf_op jit(solution)/shard_map/all_to_all | solution.py:176
  307.4 131.9 %reduce-scatter.6.cloned.1.call-start = ((), (), s32[]{:S(2)}) async-start(), calls=%async_computation.13 | async-start | bytes 3538944 | tf_op jit(solution)/shard_map/reduce_scatter | solution.py:214
  393.8 2.4 copy-start.5
  393.8 2.4 copy-start.18
  393.8 86.0 %reduce-scatter.10.cloned.1.call-start = ((), (), s32[]{:S(2)}) async-start(), calls=%async_computation.15 | async-start | bytes 655360 | tf_op jit(solution)/shard_map/reduce_scatter | solution.py:250
  395.9 117.7 %reduce-scatter.12.cloned.1.call-start = ((), (), s32[]{:S(2)}) async-start(), calls=%async_computation.16 | async-start | bytes 2621440 | tf_op jit(solution)/shard_map/reduce_scatter | solution.py:259
  398.5 160.7 %reduce-scatter.14.cloned.1.call-start = ((), (), s32[]{:S(2)}) async-start(), calls=%async_computation.17 | async-start | bytes 2621440 | tf_op jit(solution)/shard_map/reduce_scatter | solution.py:262
  401.8 194.5 %reduce-scatter.8.cloned.1.call-start = ((), (), s32[]{:S(2)}) async-start(), calls=%async_computation.14 | async-start | bytes 1966080 | tf_op jit(solution)/shard_map/reduce_scatter | solution.py:247
  479.7 116.6 %copy-start.51 = (u32[32]{0:T(128)S(1)}, u32[32]{0:T(128)}, u32[]{:S(2)}) copy-start(u32[32]{0:T(128)} %constant.143) | copy-start | bytes 388
  479.7 176.7 %all-reduce.10.cloned.1.call-start = ((), (), s32[]{:S(2)}) async-start(), calls=%async_computation.19 | async-start | bytes 2359296 | tf_op jit(solution)/shard_map/psum | solution.py:270
  559.2 130.8 %all-gather.19.cloned.1.call-start = ((), (), s32[]{:S(2)}) async-start(), calls=%async_computation.18 | async-start | bytes 3538944 | tf_op jit(solution)/shard_map/all_gather | solution.py:269
  656.4 3.9 copy-start.19
  658.1 3.3 copy-start.14
  (96 other events, 111.3 us)
Sparse Core Ops, SparseCore 0:
  10.2 40.4 all-gather.10
  85.5 31.5 all-gather.12
  118.7 46.2 all-gather.14
  166.3 50.5 all-gather.16
  393.9 45.3 reduce-scatter.5
  442.1 24.5 reduce-scatter.9
  469.1 44.5 reduce-scatter.11
  516.0 43.1 reduce-scatter.13
  561.6 34.5 reduce-scatter.7
  600.0 56.4 all-reduce.9
  658.3 31.6 all-gather.18
